TPU v7x, 32 devices: a whole 2x2x4 slice. The times are simulated.
32 devices in a mesh: lev: 2 (over x), lon: 4 (over y, core), lat: 4 (over z).
Axes of the slice: x: 2, y: 2, z: 4, core: 2. Of those that a mesh axis runs over, the one named last changes fastest.
Arguments:
- fields: bfloat16 [42, 6, 256, 512], P('lev', None, 'lat', 'lon'), may hold values from -6 to 6
- level_slot: int32 [37], replicated, may hold values from 0 to 41, as said below
- dilation: int32 [4], replicated, may hold values from 1 to 8, as said below
- lift_weight: bfloat16 [6, 128], replicated, may hold values from -2.5 to 2.5
- conv_weight: bfloat16 [4, 3, 128, 128], replicated, may hold values from -0.3125 to 0.3125
- conv_bias: float32 [4, 128], replicated, may hold values from -3 to 3
- out_weight: bfloat16 [128, 6], replicated, may hold values from -0.5 to 0.5
Outputs:
- spectra: float32 [42, 6, 2, 128, 128], P('lev', None, None, ('lon', 'lat'))
Inputs may be any that keep to these rules, and one draw needn't show every extreme that they name: level_slot rises strictly; the owner of a level is its slot // 21; owners take consecutive runs of levels; each owner holds 1 to 21 levels and some owner holds exactly 21; every owner but the last fills its first slots in order, the last owner fills its last slots in order. Some layer has dilation exactly 8.
All inputs are finite; a program needn't handle non-finite values.
Results may differ from a plain program's by a relative error of at most 0.0033.
Values may be sent and summed in bfloat16 or wider, within the bound.
A program may use at most 320 MiB of HBM per device.

v0:
```python
import math

import jax
import jax.numpy as jnp
from jax import lax
from jax.sharding import PartitionSpec as P

NLON = 512
NLAT = 256
DMAX = 8
MW = 128
NDEG = 128


def legendre_table(orders, lat_angle, degrees):
    sin_lat = jnp.sin(lat_angle)
    cos_lat = jnp.cos(lat_angle)
    counter = jnp.arange(1, degrees).astype(jnp.float32)
    log_steps = 0.5 * jnp.log((2.0 * counter + 1.0) / (2.0 * counter))
    log_table = jnp.concatenate([jnp.zeros((1,), jnp.float32), jnp.cumsum(log_steps)])
    one_hot = (orders[:, None] == jnp.arange(degrees, dtype=jnp.int32)[None, :]).astype(jnp.float32)
    log_start = jnp.sum(one_hot * log_table[None, :], axis=1)
    order_f = orders.astype(jnp.float32)[:, None]
    diagonal = jnp.sqrt(jnp.float32(0.5)) * jnp.exp(
        log_start[:, None] + order_f * jnp.log(cos_lat)[None, :]
    )
    orders_col = orders[:, None]

    def advance(carry, degree):
        prev_one, prev_two = carry
        deg_f = degree.astype(jnp.float32)
        ratio_up = jnp.sqrt(
            (4.0 * deg_f * deg_f - 1.0) / jnp.maximum(deg_f * deg_f - order_f * order_f, 1.0)
        )
        back_num = jnp.maximum((deg_f - 1.0) * (deg_f - 1.0) - order_f * order_f, 0.0)
        ratio_back = jnp.sqrt(
            back_num / jnp.maximum(4.0 * (deg_f - 1.0) * (deg_f - 1.0) - 1.0, 1.0)
        )
        recur = ratio_up * (sin_lat[None, :] * prev_one - ratio_back * prev_two)
        first = jnp.sqrt(2.0 * order_f + 3.0) * sin_lat[None, :] * prev_one
        fresh = jnp.where(
            degree == orders_col,
            diagonal,
            jnp.where(
                degree == orders_col + 1,
                first,
                jnp.where(degree > orders_col + 1, recur, jnp.zeros_like(recur)),
            ),
        )
        return ((fresh, prev_one), fresh)

    empty_rows = jnp.zeros_like(diagonal)
    final_pair, stacked = lax.scan(
        advance, (empty_rows, empty_rows), jnp.arange(degrees, dtype=jnp.int32)
    )
    return jnp.transpose(stacked, (1, 0, 2))


def latitudes(lat_ids, lat_count):
    return -0.5 * math.pi + (lat_ids.astype(jnp.float32) + 0.5) * (math.pi / lat_count)


def quad_weights(lat_angle, lat_count):
    return jnp.cos(lat_angle) * math.sqrt(2.0 * math.pi / lat_count)


def column_net(col_flat, dilation, lift_weight, conv_weight, conv_bias, out_weight):
    levels = col_flat.shape[0]
    hidden = jnp.einsum(
        "lfq,fc->lqc", col_flat, lift_weight, preferred_element_type=jnp.float32
    ).astype(jnp.bfloat16)
    for layer in range(conv_weight.shape[0]):
        spacing = dilation[layer]
        padded = jnp.pad(hidden, ((DMAX, DMAX), (0, 0), (0, 0)))
        lower_lev = lax.dynamic_slice_in_dim(padded, DMAX - spacing, levels, 0)
        upper_lev = lax.dynamic_slice_in_dim(padded, DMAX + spacing, levels, 0)
        branch_sum = (
            jnp.einsum(
                "lqc,cd->lqd", lower_lev, conv_weight[layer, 0], preferred_element_type=jnp.float32
            )
            + jnp.einsum(
                "lqc,cd->lqd", hidden, conv_weight[layer, 1], preferred_element_type=jnp.float32
            )
            + jnp.einsum(
                "lqc,cd->lqd", upper_lev, conv_weight[layer, 2], preferred_element_type=jnp.float32
            )
            + conv_bias[layer][None, None, :]
        )
        hidden = (hidden.astype(jnp.float32) + jax.nn.gelu(branch_sum, approximate=True)).astype(
            jnp.bfloat16
        )
    correction = jnp.einsum("lqc,cf->lfq", hidden, out_weight, preferred_element_type=jnp.float32)
    return (col_flat.astype(jnp.float32) + correction).astype(jnp.bfloat16)


def on_device(fields, level_slot, dilation, lift_weight, conv_weight, conv_bias, out_weight):
    slot_cap, field_count, lat_loc, lon_loc = fields.shape
    received = lax.all_to_all(fields, "lev", split_axis=3, concat_axis=0, tiled=True)
    lon_part = received.shape[3]
    columns = jnp.take(received, level_slot, axis=0)
    levels = columns.shape[0]
    col_flat = columns.reshape(levels, field_count, lat_loc * lon_part)
    corrected = column_net(col_flat, dilation, lift_weight, conv_weight, conv_bias, out_weight)
    corrected = corrected.reshape(levels, field_count, lat_loc, lon_part)
    slotted = jnp.zeros(received.shape, jnp.bfloat16).at[level_slot].set(corrected)
    level_grid = lax.all_to_all(slotted, "lev", split_axis=0, concat_axis=3, tiled=True)
    norm_scale = 1.0 / math.sqrt(NLON)
    circle = lax.all_to_all(level_grid, "lon", split_axis=2, concat_axis=3, tiled=True)
    sub_rows = circle.shape[2]
    circle_wide = circle.astype(jnp.float32)
    every_wave = jnp.arange(MW, dtype=jnp.int32)
    every_lon = jnp.arange(NLON, dtype=jnp.int32)
    phase_all = (every_wave[:, None] * every_lon[None, :] % NLON).astype(jnp.float32) * (
        2.0 * math.pi / NLON
    )
    cos_all = jnp.cos(phase_all) * norm_scale
    sin_all = -jnp.sin(phase_all) * norm_scale
    real_all = jnp.einsum("sflx,mx->msfl", circle_wide, cos_all, precision=lax.Precision.HIGHEST)
    imag_all = jnp.einsum("sflx,mx->msfl", circle_wide, sin_all, precision=lax.Precision.HIGHEST)
    fourier_all = jnp.stack([real_all, imag_all], axis=1)
    lat_groups = lax.axis_size("lat")
    position = jnp.arange(NLAT, dtype=jnp.int32)
    source_id = position // sub_rows
    within = position % sub_rows
    source_lon = source_id // lat_groups
    source_lat = source_id % lat_groups
    order_ids = source_lat * lat_loc + source_lon * sub_rows + within
    order_angle = latitudes(order_ids, NLAT)
    order_weight = quad_weights(order_angle, NLAT)
    owner_index = lax.axis_index("lon") * lat_groups + lax.axis_index("lat")
    coef_part = lax.all_to_all(fourier_all, ("lon", "lat"), split_axis=0, concat_axis=4, tiled=True)
    own_count = coef_part.shape[0]
    wave_ids = owner_index * own_count + jnp.arange(own_count, dtype=jnp.int32)
    leg_table = legendre_table(wave_ids, order_angle, NDEG) * order_weight[None, None, :]
    return jnp.einsum("mnk,mrsfk->sfrmn", leg_table, coef_part, precision=lax.Precision.HIGHEST)


def solution(mesh):
    placed = (P("lev", None, "lat", "lon"), P(), P(), P(), P(), P(), P())
    return jax.shard_map(
        on_device,
        mesh=mesh,
        in_specs=placed,
        out_specs=P("lev", None, None, ("lon", "lat"), None),
        check_vma=False,
    )
```

profile of v0, /device:TPU:0, one launch (start us, length us, event | category | flops | bytes accessed | tf_op | source)
XLA Modules:
  0.0 1372.5 jit_solution(2322952316868844590)
XLA Ops:
  0.0 6.2 copy.72
  6.2 5.5 reshape.353
  11.7 4.2 all-to-all-start
  15.9 1.5 fusion.167
  29.0 1.4 slice_bitcast_fusion
  30.4 11.0 all-to-all-done
  41.4 5.4 reshape.354
  46.8 13.5 copy.93
  60.3 5.3 copy.74
  65.6 5.2 gather_fusion
  70.8 5.3 reshape.347
  76.2 19.3 %convolution_convert_fusion = bf16[37,4096,128]{2,1,0:T(8,128)(2,1)} fusion(bf16[37,6,4096]{2,1,0:T(8,128)(2,1)S(1)} %reshape.347, pred[37]{0:T(512)(128)(4,1)S(1)} %compare_and_fusion, bf16[6,128]{1,0:T(8,128)(2,1)S(1)} %copy-done), kind=kOutput, calls=%fused_computation.98 | convolution fusion | flops 253091840 | bytes 40617508 | tf_op jit(solution)/shard_map/lfq,fc->lqc/dot_general | solution.py:69
  95.5 38.2 %fusion.104 = f32[37,4096,128]{2,1,0:T(8,128)} fusion(bf16[37,4096,128]{2,1,0:T(8,128)(2,1)} %convolution_convert_fusion, bf16[4,3,128,128]{3,2,1,0:T(8,128)(2,1)S(1)} %copy-done.5), kind=kOutput, calls=%fused_computation.143 | convolution fusion | flops 4966055936 | bytes 116424704 | tf_op jit(solution)/shard_map/lqc,cd->lqd/dot_general | solution.py:81
  133.7 40.4 %fusion.61 = f32[37,4096,128]{2,1,0:T(8,128)} fusion(s32[]{:T(128)S(6)} %select_n.144, bf16[37,4096,128]{2,1,0:T(8,128)(2,1)} %convolution_convert_fusion, bf16[4,3,128,128]{3,2,1,0:T(8,128)(2,1)S(1)} %copy-done.5), kind=kOutput, calls=%fused_computation.91 | convolution fusion | flops 4966055936 | bytes 116424704 | tf_op jit(solution)/shard_map/lqc,cd->lqd/dot_general | solution.py:84
  174.1 84.6 %fusion.32 = bf16[37,4096,128]{2,1,0:T(8,128)(2,1)} fusion(f32[37,4096,128]{2,1,0:T(8,128)} %fusion.61, f32[37,4096,128]{2,1,0:T(8,128)} %fusion.104, bf16[37,4096,128]{2,1,0:T(8,128)(2,1)} %convolution_convert_fusion, s32[]{:T(128)S(6)} %select_n.143, f32[128]{0:T(128)S(1)} %get-tuple-element.310, bf16[4,3,128,128]{3,2,1,0:T(8,128)(2,1)S(1)} %copy-done.5), kind=kOutput, calls=%fused_computation.54 | convolution fusion | flops 5237637120 | bytes 271614464 | tf_op jit(solution)/shard_map/lqc,cd->lqd/dot_general | solution.py:78
  258.7 38.2 %fusion.100 = f32[37,4096,128]{2,1,0:T(8,128)} fusion(bf16[37,4096,128]{2,1,0:T(8,128)(2,1)} %fusion.32, bf16[4,3,128,128]{3,2,1,0:T(8,128)(2,1)S(1)} %copy-done.5), kind=kOutput, calls=%fused_computation.139 | convolution fusion | flops 4966055936 | bytes 116424704 | tf_op jit(solution)/shard_map/lqc,cd->lqd/dot_general | solution.py:81
  296.9 39.4 %fusion.63 = f32[37,4096,128]{2,1,0:T(8,128)} fusion(s32[]{:T(128)S(6)} %select_n.146, bf16[37,4096,128]{2,1,0:T(8,128)(2,1)} %fusion.32, bf16[4,3,128,128]{3,2,1,0:T(8,128)(2,1)S(1)} %copy-done.5), kind=kOutput, calls=%fused_computation.93 | convolution fusion | flops 4966055936 | bytes 116424704 | tf_op jit(solution)/shard_map/lqc,cd->lqd/dot_general | solution.py:84
  336.3 83.2 %fusion.41 = bf16[37,4096,128]{2,1,0:T(8,128)(2,1)} fusion(f32[37,4096,128]{2,1,0:T(8,128)} %fusion.63, f32[37,4096,128]{2,1,0:T(8,128)} %fusion.100, bf16[37,4096,128]{2,1,0:T(8,128)(2,1)} %fusion.32, s32[]{:T(128)S(6)} %select_n.145, f32[128]{0:T(128)S(1)} %copy-done.12, bf16[4,3,128,128]{3,2,1,0:T(8,128)(2,1)S(1)} %copy-done.5), kind=kOutput, calls=%fused_computation.63 | convolution fusion | flops 5237637120 | bytes 271614464 | tf_op jit(solution)/shard_map/lqc,cd->lqd/dot_general | solution.py:78
  419.5 38.2 %fusion.96 = f32[37,4096,128]{2,1,0:T(8,128)} fusion(bf16[37,4096,128]{2,1,0:T(8,128)(2,1)} %fusion.41, bf16[4,3,128,128]{3,2,1,0:T(8,128)(2,1)S(1)} %copy-done.5), kind=kOutput, calls=%fused_computation.135 | convolution fusion | flops 4966055936 | bytes 116424704 | tf_op jit(solution)/shard_map/lqc,cd->lqd/dot_general | solution.py:81
  457.6 38.6 %fusion.65 = f32[37,4096,128]{2,1,0:T(8,128)} fusion(s32[]{:T(128)S(6)} %select_n.148, bf16[37,4096,128]{2,1,0:T(8,128)(2,1)} %fusion.41, bf16[4,3,128,128]{3,2,1,0:T(8,128)(2,1)S(1)} %copy-done.5), kind=kOutput, calls=%fused_computation.95 | convolution fusion | flops 4966055936 | bytes 116424704 | tf_op jit(solution)/shard_map/lqc,cd->lqd/dot_general | solution.py:84
  496.3 82.5 %fusion.50 = bf16[37,4096,128]{2,1,0:T(8,128)(2,1)} fusion(f32[37,4096,128]{2,1,0:T(8,128)} %fusion.65, f32[37,4096,128]{2,1,0:T(8,128)} %fusion.96, bf16[37,4096,128]{2,1,0:T(8,128)(2,1)} %fusion.41, s32[]{:T(128)S(6)} %select_n.147, f32[128]{0:T(128)S(1)} %copy-done.11, bf16[4,3,128,128]{3,2,1,0:T(8,128)(2,1)S(1)} %copy-done.5), kind=kOutput, calls=%fused_computation.72 | convolution fusion | flops 5237637120 | bytes 271614464 | tf_op jit(solution)/shard_map/lqc,cd->lqd/dot_general | solution.py:78
  578.8 38.2 %fusion.91 = f32[37,4096,128]{2,1,0:T(8,128)} fusion(bf16[37,4096,128]{2,1,0:T(8,128)(2,1)} %fusion.50, bf16[4,3,128,128]{3,2,1,0:T(8,128)(2,1)S(1)} %copy-done.5), kind=kOutput, calls=%fused_computation.131 | convolution fusion | flops 4966055936 | bytes 116424704 | tf_op jit(solution)/shard_map/lqc,cd->lqd/dot_general | solution.py:81
  617.0 39.3 %fusion.67 = f32[37,4096,128]{2,1,0:T(8,128)} fusion(s32[]{:T(128)S(6)} %select_n.150, bf16[37,4096,128]{2,1,0:T(8,128)(2,1)} %fusion.50, bf16[4,3,128,128]{3,2,1,0:T(8,128)(2,1)S(1)} %copy-done.5), kind=kOutput, calls=%fused_computation.97 | convolution fusion | flops 4966055936 | bytes 116424704 | tf_op jit(solution)/shard_map/lqc,cd->lqd/dot_general | solution.py:84
  656.3 71.7 %fusion.69 = bf16[37,6,4096]{2,1,0:T(8,128)(2,1)} fusion(f32[37,4096,128]{2,1,0:T(8,128)} %fusion.67, f32[37,4096,128]{2,1,0:T(8,128)} %fusion.91, bf16[37,4096,128]{2,1,0:T(8,128)(2,1)} %fusion.50, s32[]{:T(128)S(6)} %select_n.149, f32[128]{0:T(128)S(1)} %copy-done.10, bf16[37,6,4096]{2,1,0:T(8,128)(2,1)S(1)} %copy-done.3, ...), kind=kOutput, calls=%fused_computation.101 | convolution fusion | flops 5474058240 | bytes 237063168 | tf_op jit(solution)/shard_map/lqc,cf->lfq/dot_general | solution.py:92
  728.1 6.5 reshape.348
  734.6 3.0 broadcast_in_dim.72
  737.6 12.6 scatter_fusion
  750.2 4.8 reshape.355
  755.0 27.9 %all_to_all.72 = bf16[2,2,258048]{2,1,0:T(2,128)(2,1)} all-to-all(bf16[2,2,258048]{2,1,0:T(2,128)(2,1)S(1)} %reshape.355), channel_id=1, replica_groups=mesh['lev'=2,'lon'=4,'lat'=4] {'lev'}, dimensions={0} | all-to-all | bytes 4128768 | tf_op jit(solution)/shard_map/all_to_all | solution.py:106
  782.9 5.6 reshape.356
  788.5 8.4 copy.96
  796.8 8.2 reshape.349
  805.0 3.8 all-to-all-start.2
  809.5 27.7 %all-to-all-done.2 = bf16[21,6,64,128]{3,0,1,2:T(8,128)(2,1)S(1)} async-done(((bf16[21,6,64,128]{3,0,1,2:T(8,128)(2,1)}), bf16[21,6,64,128]{3,0,1,2:T(8,128)(2,1)S(1)}, u32[]{:S(2)}, u32[]{:S(2)}) %all-to-all-start.2) | async-done | bytes 2064416 | tf_op jit(solution)/shard_map/all_to_all | solution.py:108
  837.3 4.0 copy.102
  841.3 3.8 reshape.351
  845.1 3.1 convolution_bitcast_fusion.2
  848.1 3.0 convolution_bitcast_fusion.3
  851.3 10.9 copy.85
  862.2 13.5 reshape.357
  875.7 5.2 all-to-all-start.3
  881.0 426.9 %while.21 = (s32[]{:T(128)}, f32[8,256]{1,0:T(8,128)S(1)}, f32[8,256]{1,0:T(8,128)S(1)}, f32[128,8,256]{2,1,0:T(8,128)}, s32[128]{0:T(128)S(1)}, /*index=5*/s32[...) while((s32[]{:T(128)}, f32[8,256]{1,0:T(8,128)S(1)}, ...), condition=%wide.region_4.5_spmd.clone.clone.clone.clone, body=%wide.region_3.4_spmd.clone.clone.clone.clone.sunk | while | flops 36782 | bytes 45171 | solution.py:53
  1311.0 7.3 reduce.1
  1318.3 20.0 %reshape.358 = f32[128,2,6,16,21]{4,3,2,1,0:T(8,128)} reshape(f32[16,32256]{1,0:T(8,128)S(1)} %reduce.1) | data formatting | bytes 4128768
  1338.3 17.9 %copy.98 = f32[8,2,21,6,16,16]{5,4,2,3,1,0:T(8,128)} copy(f32[8,2,21,6,16,16]{2,5,3,1,0,4:T(8,128)} %bitcast.186) | data formatting | bytes 4128768 | tf_op jit(solution)/shard_map/all_to_all | solution.py:131
  1356.2 11.8 reshape.350
  1368.1 2.4 convolution_bitcast_fusion.1
  1370.5 1.6 copy.89
  (942 shorter events, 346.0 us)
Async XLA Ops:
  0.0 76.2 %copy-start = (bf16[6,128]{1,0:T(8,128)(2,1)S(1)}, bf16[6,128]{1,0:T(8,128)(2,1)}, u32[]{:S(2)}) copy-start(bf16[6,128]{1,0:T(8,128)(2,1)} %param.12) | copy-start | bytes 4612
  11.7 29.7 %all-to-all-start = ((bf16[2,2,258048]{2,1,0:T(2,128)(2,1)}), bf16[2,2,258048]{2,1,0:T(2,128)(2,1)S(1)}, u32[]{:S(2)}, u32[]{:S(2)}) async-start(bf16[2,2,258048]{2,1,0:T(2,128)(2,1)} %reshape.353), calls=%async_computation | async-start | bytes 4128768 | tf_op jit(solution)/shard_map/all_to_all | solution.py:98
  28.3 0.7 copy-start.8
  29.0 66.5 %copy-start.6 = (pred[37]{0:T(512)(128)(4,1)}, pred[37]{0:T(512)(128)(4,1)S(1)}, u32[]{:S(2)}) copy-start(pred[37]{0:T(512)(128)(4,1)S(1)} %compare_and_fusion) | copy-start | bytes 115
  60.3 35.2 %copy-start.5 = (bf16[4,3,128,128]{3,2,1,0:T(8,128)(2,1)S(1)}, bf16[4,3,128,128]{3,2,1,0:T(8,128)(2,1)}, u32[]{:S(2)}) copy-start(bf16[4,3,128,128]{3,2,1,0:T(8,128)(2,1)} %param.13) | copy-start | bytes 1179652
  76.2 57.5 %copy-start.2 = (bf16[37,6,4096]{2,1,0:T(8,128)(2,1)}, bf16[37,6,4096]{2,1,0:T(8,128)(2,1)S(1)}, u32[]{:S(2)}) copy-start(bf16[37,6,4096]{2,1,0:T(8,128)(2,1)S(1)} %reshape.347) | copy-start | bytes 5455876
  296.9 39.4 %copy-start.12 = (f32[128]{0:T(128)S(1)}, f32[128]{0:T(128)}, u32[]{:S(2)}) copy-start(f32[128]{0:T(128)} %get-tuple-element.309) | copy-start | bytes 1540
  457.6 38.6 %copy-start.11 = (f32[128]{0:T(128)S(1)}, f32[128]{0:T(128)}, u32[]{:S(2)}) copy-start(f32[128]{0:T(128)} %get-tuple-element.311) | copy-start | bytes 1540
  617.0 39.3 %copy-start.3 = (bf16[37,6,4096]{2,1,0:T(8,128)(2,1)S(1)}, bf16[37,6,4096]{2,1,0:T(8,128)(2,1)}, u32[]{:S(2)}) copy-start(bf16[37,6,4096]{2,1,0:T(8,128)(2,1)} %copy-done.2) | copy-start | bytes 5455876
  617.0 39.3 %copy-start.7 = (pred[37]{0:T(512)(128)(4,1)S(1)}, pred[37]{0:T(512)(128)(4,1)}, u32[]{:S(2)}) copy-start(pred[37]{0:T(512)(128)(4,1)} %copy-done.6) | copy-start | bytes 115
  617.0 39.3 %copy-start.10 = (f32[128]{0:T(128)S(1)}, f32[128]{0:T(128)}, u32[]{:S(2)}) copy-start(f32[128]{0:T(128)} %get-tuple-element.308) | copy-start | bytes 1540
  617.0 39.3 %copy-start.13 = (bf16[128,6]{0,1:T(8,128)(2,1)S(1)}, bf16[128,6]{0,1:T(8,128)(2,1)}, u32[]{:S(2)}) copy-start(bf16[128,6]{0,1:T(8,128)(2,1)} %param.15) | copy-start | bytes 4612
  656.3 81.2 %copy-start.9 = (s32[37]{0:T(128)S(1)}, s32[37]{0:T(128)}, u32[]{:S(2)}) copy-start(s32[37]{0:T(128)} %copy-done.8) | copy-start | bytes 448
  805.0 32.2 %all-to-all-start.2 = ((bf16[21,6,64,128]{3,0,1,2:T(8,128)(2,1)}), bf16[21,6,64,128]{3,0,1,2:T(8,128)(2,1)S(1)}, u32[]{:S(2)}, u32[]{:S(2)}) async-start(bf16[21,6,64,128]{3,0,1,2:T(8,128)(2,1)} %reshape.349), calls=%async_computation.2 | async-start | bytes 4718592 | tf_op jit(solution)/shard_map/all_to_all | solution.py:108
  875.7 433.4 %all-to-all-start.3 = ((f32[16,1,32256]{2,1,0:T(1,128)}), f32[16,1,32256]{2,1,0:T(1,128)S(1)}, u32[]{:S(2)}, u32[]{:S(2)}) async-start(f32[16,1,32256]{2,1,0:T(1,128)} %reshape.357), calls=%async_computation.3 | async-start | bytes 4128768 | tf_op jit(solution)/shard_map/all_to_all | solution.py:131
  880.9 491.1 %copy-start.1 = (bf16[6,128]{1,0:T(8,128)(2,1)S(1)}, bf16[6,128]{1,0:T(8,128)(2,1)}, u32[]{:S(2)}) copy-start(bf16[6,128]{1,0:T(8,128)(2,1)} %param.12) | copy-start | bytes 4612
  1309.1 1.3 copy-start.4
where the time goes:
time: 1390 us; the launch traced here: 1370 us
  matrix products  660 us (47%)
  other arithmetic  273 us (20%)
  local copies, waits for them, and re-layouts  263 us (19%)
  loops' own time  86.2 us (6%)
  waiting for transfers between devices  38.7 us (3%)
  blocking collectives  27.9 us (2%)
    dot_general x3, matrix products, column_net(): jnp.einsum('lqc,cd->lqd', lower_lev, conv_weight[layer, 0], preferred_ele...  250 us
    dot_general x4, matrix products, column_net(): jnp.einsum('lqc,cd->lqd', upper_lev, conv_weight[layer, 2], preferred_ele...  158 us
    dot_general x4, matrix products, column_net(): jnp.einsum('lqc,cd->lqd', hidden, conv_weight[layer, 1], preferred_elemen...  153 us
    dynamic_update_slice x128, other arithmetic, legendre_table(): lax.scan(advance, (empty_rows, empty_rows), jnp.arange(degrees, dtype=jnp...  87.5 us
    another operation x1, loops' own time, legendre_table(): lax.scan(advance, (empty_rows, empty_rows), jnp.arange(degrees, dtype=jnp...  86.2 us
    gt x128, other arithmetic, advance(): degree > orders_col + 1  82.3 us
    eq x128, other arithmetic, advance(): degree == orders_col  81.4 us
    dynamic_slice x128, local copies, waits for them, and re-layouts, legendre_table(): lax.scan(advance, (empty_rows, empty_rows), jnp.arange(degrees, dtype=jnp...  78.8 us
  transfers between devices with their start and end apart: 3, of which 2 were waited for; matrix products, arithmetic and copies ran while one was open for 25% of the time, Pallas kernels for 0%

commit v1 on v0

v1 whole, which is shorter than its diff:
```python
import math

import jax
import jax.numpy as jnp
import numpy as np
from jax import lax
from jax.experimental import pallas as pl
from jax.experimental.pallas import tpu as pltpu
from jax.sharding import PartitionSpec as P

NLON = 512
NLAT = 256
DMAX = 8
MW = 128
NDEG = 128


def legendre_table(orders, lat_angle, degrees):
    sin_lat = jnp.sin(lat_angle)
    cos_lat = jnp.cos(lat_angle)
    counter = jnp.arange(1, degrees).astype(jnp.float32)
    log_steps = 0.5 * jnp.log((2.0 * counter + 1.0) / (2.0 * counter))
    log_table = jnp.concatenate([jnp.zeros((1,), jnp.float32), jnp.cumsum(log_steps)])
    one_hot = (orders[:, None] == jnp.arange(degrees, dtype=jnp.int32)[None, :]).astype(jnp.float32)
    log_start = jnp.sum(one_hot * log_table[None, :], axis=1)
    order_f = orders.astype(jnp.float32)[:, None]
    diagonal = jnp.sqrt(jnp.float32(0.5)) * jnp.exp(
        log_start[:, None] + order_f * jnp.log(cos_lat)[None, :]
    )
    count, lats = diagonal.shape
    order_full = jnp.broadcast_to(order_f, (count, lats))
    sin_full = jnp.broadcast_to(sin_lat[None, :], (count, lats))
    return pl.pallas_call(
        legendre_kernel,
        out_shape=jax.ShapeDtypeStruct((degrees, count, lats), jnp.float32),
        name="legendre",
    )(order_full, sin_full, diagonal)


def legendre_kernel(order_ref, sin_ref, diag_ref, out_ref):
    order = order_ref[...]
    sin_lat = sin_ref[...]
    diagonal = diag_ref[...]
    first_scale = jnp.sqrt(2.0 * order + 3.0) * sin_lat
    zero = order * 0.0

    def advance(degree, carry):
        prev_one, prev_two = carry
        deg = zero + degree.astype(jnp.float32)
        ratio_up = jnp.sqrt((4.0 * deg * deg - 1.0) / jnp.maximum(deg * deg - order * order, 1.0))
        before = deg - 1.0
        back_num = jnp.maximum(before * before - order * order, 0.0)
        ratio_back = jnp.sqrt(back_num / jnp.maximum(4.0 * before * before - 1.0, 1.0))
        recur = ratio_up * (sin_lat * prev_one - ratio_back * prev_two)
        first = first_scale * prev_one
        fresh = jnp.where(
            deg == order,
            diagonal,
            jnp.where(deg == order + 1.0, first, jnp.where(deg > order + 1.0, recur, zero)),
        )
        out_ref[degree] = fresh
        return fresh, prev_one

    lax.fori_loop(0, out_ref.shape[0], advance, (zero, zero))


def latitudes(lat_ids, lat_count):
    return -0.5 * math.pi + (lat_ids.astype(jnp.float32) + 0.5) * (math.pi / lat_count)


def quad_weights(lat_angle, lat_count):
    return jnp.cos(lat_angle) * math.sqrt(2.0 * math.pi / lat_count)


def column_kernel(dil_ref, col_ref, lift_ref, conv_ref, bias_ref, out_w_ref, out_ref, ping, pong):
    levels, _, tile = col_ref.shape
    channels = lift_ref.shape[1]
    layers = conv_ref.shape[0]

    @pl.when(pl.program_id(0) == 0)
    def _():
        edge = jnp.zeros((DMAX, tile, channels), jnp.bfloat16)
        for buf in (ping, pong):
            buf[pl.ds(0, DMAX)] = edge
            buf[pl.ds(DMAX + levels, DMAX)] = edge

    lift = lift_ref[...]

    def lift_level(lev, carry):
        hidden = lax.dot_general(
            col_ref[lev], lift, (((0,), (0,)), ((), ())), preferred_element_type=jnp.float32
        )
        ping[DMAX + lev] = hidden.astype(jnp.bfloat16)
        return carry

    lax.fori_loop(0, levels, lift_level, 0)

    inner = math.sqrt(2.0 / math.pi)
    for layer in range(layers):
        src, dst = (ping, pong) if layer % 2 == 0 else (pong, ping)
        spacing = dil_ref[layer]

        def conv_level(lev, carry, src=src, dst=dst, spacing=spacing, layer=layer):
            own = src[DMAX + lev]
            taps = jnp.concatenate(
                [src[DMAX + lev - spacing], own, src[DMAX + lev + spacing]], axis=1
            )
            value = (
                jnp.dot(taps, conv_ref[layer], preferred_element_type=jnp.float32)
                + bias_ref[pl.ds(layer, 1), :]
            )
            curve = jnp.tanh(value * (inner + (inner * 0.044715) * (value * value)))
            half = 0.5 * value
            fresh = (own.astype(jnp.float32) + (half + half * curve)).astype(jnp.bfloat16)
            if layer + 1 < layers:
                dst[DMAX + lev] = fresh
            else:
                correction = lax.dot_general(
                    out_w_ref[...], fresh, (((1,), (1,)), ((), ())),
                    preferred_element_type=jnp.float32,
                )
                out_ref[lev] = (col_ref[lev].astype(jnp.float32) + correction).astype(jnp.bfloat16)
            return carry

        lax.fori_loop(0, levels, conv_level, 0)


def column_net(col_flat, dilation, lift_weight, conv_weight, conv_bias, out_weight):
    levels, field_count, columns = col_flat.shape
    layers, taps, channels, _ = conv_weight.shape
    tile = min(512, columns)
    while columns % tile:
        tile //= 2
    whole = lambda *dims: pl.BlockSpec(dims, lambda i, d: (0,) * len(dims))
    moving = pl.BlockSpec((levels, field_count, tile), lambda i, d: (0, 0, i))
    scratch = pltpu.VMEM((levels + 2 * DMAX, tile, channels), jnp.bfloat16)
    return pl.pallas_call(
        column_kernel,
        out_shape=jax.ShapeDtypeStruct(col_flat.shape, jnp.bfloat16),
        grid_spec=pltpu.PrefetchScalarGridSpec(
            num_scalar_prefetch=1,
            grid=(columns // tile,),
            in_specs=[
                moving,
                whole(field_count, channels),
                whole(layers, taps * channels, channels),
                whole(layers, channels),
                whole(field_count, channels),
            ],
            out_specs=moving,
            scratch_shapes=[scratch, scratch],
        ),
        compiler_params=pltpu.CompilerParams(vmem_limit_bytes=48 * 1024 * 1024),
        name="column_net",
    )(
        dilation,
        col_flat,
        lift_weight,
        conv_weight.reshape(layers, taps * channels, channels),
        conv_bias,
        jnp.transpose(out_weight),
    )


def on_device(fields, level_slot, dilation, lift_weight, conv_weight, conv_bias, out_weight):
    slot_cap, field_count, lat_loc, lon_loc = fields.shape
    received = lax.all_to_all(fields, "lev", split_axis=3, concat_axis=0, tiled=True)
    lon_part = received.shape[3]
    columns = jnp.take(received, level_slot, axis=0)
    levels = columns.shape[0]
    col_flat = columns.reshape(levels, field_count, lat_loc * lon_part)
    corrected = column_net(col_flat, dilation, lift_weight, conv_weight, conv_bias, out_weight)
    corrected = corrected.reshape(levels, field_count, lat_loc, lon_part)
    slotted = jnp.zeros(received.shape, jnp.bfloat16).at[level_slot].set(corrected)
    level_grid = lax.all_to_all(slotted, "lev", split_axis=0, concat_axis=3, tiled=True)
    norm_scale = 1.0 / math.sqrt(NLON)
    lat_groups = lax.axis_size("lat")
    lon_groups = lax.axis_size("lon")
    owners = lat_groups * lon_groups
    owner_index = lax.axis_index("lon") * lat_groups + lax.axis_index("lat")
    rows = jnp.transpose(
        level_grid.reshape(slot_cap * field_count, lat_loc, lon_loc), (1, 0, 2)
    )
    circle = lax.all_to_all(rows, "lon", split_axis=0, concat_axis=2, tiled=True)
    sub_rows = circle.shape[0]
    waves = np.arange(MW, dtype=np.int64)[:, None] * np.arange(NLON, dtype=np.int64)[None, :] % NLON
    phase = waves.astype(np.float64) * (2.0 * math.pi / NLON)
    table = np.stack([np.cos(phase), -np.sin(phase)], axis=1).reshape(2 * MW, NLON) * norm_scale
    table_high = table.astype(jnp.bfloat16)
    table_low = (table - table_high.astype(np.float64)).astype(jnp.bfloat16)
    wide = lambda part: jnp.einsum(
        "wx,lcx->wlc", jnp.asarray(part), circle, preferred_element_type=jnp.float32
    )
    fourier = (wide(table_high) + wide(table_low)).astype(jnp.bfloat16)
    own_count = MW // owners
    fourier = fourier.reshape(owners, own_count, 2, sub_rows, slot_cap * field_count)
    coef = lax.all_to_all(fourier, ("lon", "lat"), split_axis=0, concat_axis=0, tiled=True)
    position = jnp.arange(NLAT, dtype=jnp.int32)
    source_id = position // sub_rows
    within = position % sub_rows
    source_lon = source_id // lat_groups
    source_lat = source_id % lat_groups
    order_ids = source_lat * lat_loc + source_lon * sub_rows + within
    order_angle = latitudes(order_ids, NLAT)
    order_weight = quad_weights(order_angle, NLAT)
    wave_ids = owner_index * own_count + jnp.arange(own_count, dtype=jnp.int32)
    leg_table = legendre_table(wave_ids, order_angle, NDEG) * order_weight[None, None, :]
    leg_rows = jnp.transpose(leg_table, (1, 0, 2))
    leg_high = leg_rows.astype(jnp.bfloat16)
    leg_low = (leg_rows - leg_high.astype(jnp.float32)).astype(jnp.bfloat16)
    coef = jnp.transpose(coef, (1, 2, 4, 0, 3)).reshape(
        own_count, 2 * slot_cap * field_count, NLAT
    )
    both = jnp.concatenate([leg_high, leg_low], axis=1)
    sums = jnp.einsum("mck,mnk->mcn", coef, both, preferred_element_type=jnp.float32)
    spectra = (sums[..., :NDEG] + sums[..., NDEG:]).reshape(
        own_count, 2, slot_cap, field_count, NDEG
    )
    return jnp.transpose(spectra, (2, 3, 1, 0, 4))


def solution(mesh):
    placed = (P("lev", None, "lat", "lon"), P(), P(), P(), P(), P(), P())
    return jax.shard_map(
        on_device,
        mesh=mesh,
        in_specs=placed,
        out_specs=P("lev", None, None, ("lon", "lat"), None),
        check_vma=False,
    )
```

time: 1390 us -> 702 us (0.51); the launches traced: 1370 us -> 701 us
  matrix products: 660 us -> 2.06 us
  Pallas kernels: 0 us -> 478 us
  other arithmetic: 273 us -> 4.64 us
  local copies, waits for them, and re-layouts: 263 us -> 109 us
  loops' own time: 86.2 us -> 0 us
  blocking collectives: 27.9 us -> 56.5 us
    dot_general x16 -> x3, matrix products: 660 us -> 2.06 us  [the longest x2 1.53 us: on_device(): jnp.einsum('wx,lcx->wlc', jnp.asarray(part), circle, preferred_element_ty...]
    pallas_call x0 -> x2, Pallas kernels: none -> 478 us  [the longest x1 472 us: column_net(): pl.pallas_call(column_kernel, out_shape=jax.ShapeDtypeStruct(col_flat.sha...]
    dynamic_update_slice x128 -> x0, other arithmetic: 87.5 us -> none  [legendre_table(): lax.scan(advance, (empty_rows, empty_rows), jnp.arange(degrees, dtype=jnp...]
    another operation x1 -> x0, loops' own time: 86.2 us -> none  [legendre_table(): lax.scan(advance, (empty_rows, empty_rows), jnp.arange(degrees, dtype=jnp...]
    gt x128 -> x0, other arithmetic: 82.3 us -> none  [advance(): degree > orders_col + 1]
    eq x128 -> x0, other arithmetic: 81.4 us -> none  [advance(): degree == orders_col]
    dynamic_slice x128 -> x0, local copies, waits for them, and re-layouts: 78.8 us -> none  [legendre_table(): lax.scan(advance, (empty_rows, empty_rows), jnp.arange(degrees, dtype=jnp...]
    all_to_all x5 -> x1, local copies, waits for them, and re-layouts: 38 us -> 3.16 us  [on_device(): lax.all_to_all(rows, 'lon', split_axis=0, concat_axis=2, tiled=True)]
  transfers between devices with their start and end apart: 3 -> 2, of which waited for: 2 -> 2; matrix products, arithmetic and copies ran while one was open for 25% -> 1% of each run, Pallas kernels for 0% -> 1%
where the time goes in v1:
time: 702 us; the launch traced here: 701 us
  Pallas kernels  478 us (68%)
  local copies, waits for them, and re-layouts  109 us (16%)
  blocking collectives  56.5 us (8%)
  waiting for transfers between devices  41.5 us (6%)
  starting transfers between devices  9.32 us (1%)
    pallas_call x1, Pallas kernels, column_net(): pl.pallas_call(column_kernel, out_shape=jax.ShapeDtypeStruct(col_flat.sha...  472 us
    all_to_all x1, blocking collectives, on_device(): lax.all_to_all(rows, 'lon', split_axis=0, concat_axis=2, tiled=True)  28.9 us
    unnamed x21, local copies, waits for them, and re-layouts  28.2 us
    all_to_all x1, blocking collectives, on_device(): lax.all_to_all(slotted, 'lev', split_axis=0, concat_axis=3, tiled=True)  27.6 us
    all_to_all x1, waiting for transfers between devices, on_device(): lax.all_to_all(fields, 'lev', split_axis=3, concat_axis=0, tiled=True)  25.5 us
    all_to_all x2, local copies, waits for them, and re-layouts, on_device(): lax.all_to_all(fields, 'lev', split_axis=3, concat_axis=0, tiled=True)  18.7 us
    all_to_all x1, waiting for transfers between devices, on_device(): lax.all_to_all(fourier, ('lon', 'lat'), split_axis=0, concat_axis=0, tile...  16 us
  transfers between devices with their start and end apart: 2, of which 2 were waited for; matrix products, arithmetic and copies ran while one was open for 1% of the time, Pallas kernels for 1%

profile of v1, /device:TPU:0, one launch (start us, length us, event | category | flops | bytes accessed | tf_op | source)
XLA Modules:
  0.0 700.6 jit_solution(7158107150544794032)
XLA Ops:
  0.0 6.2 copy.78
  6.2 5.5 reshape.225
  11.7 4.4 all-to-all-start
  16.1 25.5 %all-to-all-done = bf16[2,2,258048]{2,1,0:T(2,128)(2,1)S(1)} async-done(((bf16[2,2,258048]{2,1,0:T(2,128)(2,1)}), bf16[2,2,258048]{2,1,0:T(2,128)(2,1)S(1)}, u32[]{:S(2)}, u32[]{:S(2)}) %all-to-all-start) | async-done | bytes 2064416 | tf_op jit(solution)/shard_map/all_to_all | solution.py:167
  41.6 5.3 reshape.226
  46.9 13.5 %copy.100 = bf16[21,6,64,2,64]{4,3,2,1,0:T(2,128)(2,1)} copy(bf16[21,6,64,2,64]{2,0,1,4,3:T(8,128)(2,1)} %bitcast.42) | data formatting | bytes 4128768 | tf_op jit(solution)/shard_map/all_to_all | solution.py:167
  60.4 5.2 copy.80
  65.6 5.3 gather_fusion
  70.9 5.3 reshape.222
  76.3 0.4 broadcast_select_fusion.col_ref
  76.7 0.6 copy-done
  77.3 472.2 %column_net.1 = bf16[37,6,4096]{2,1,0:T(8,128)(2,1)S(1)} custom-call(s32[4]{0:T(128)S(1)} %copy-done.4, bf16[37,6,4096]{2,1,0:T(8,128)(2,1)S(1)} %broadcast_select_fusion.col_ref, bf16[6,128]{1,0:T(8,128)(2,1)S(1)} %copy-done.1, bf16[4,384,128]{2,1,0:T(8,128)(2,1)S(1)} %bitcast.40, f32[4,128]{1,0:T(4,128)S(1)} %copy-done.2, bf16[6,128]{1,0:T(8,128)(2,1)S(1)} %bitcast.41), custom_call_target="tpu_custom_call" | custom-call | tf_op jit(solution)/shard_map/column_net/pallas_call | solution.py:137
  549.5 5.5 reshape.223
  555.0 3.0 broadcast_in_dim.18
  558.0 12.6 %scatter_fusion = bf16[42,6,64,64]{3,2,1,0:T(8,128)(2,1)} fusion(bf16[42,6,64,64]{3,2,1,0:T(8,128)(2,1)} %broadcast_in_dim.18, s32[37]{0:T(128)S(1)} %compare_select_fusion, bf16[37,6,64,64]{3,2,1,0:T(8,128)(2,1)} %reshape.223), kind=kCustom, calls=%fused_computation.1 | custom fusion | bytes 5456020 | tf_op jit(solution)/shard_map/scatter | solution.py:174
  570.6 4.8 reshape.227
  575.4 27.6 %all_to_all.56 = bf16[2,2,258048]{2,1,0:T(2,128)(2,1)} all-to-all(bf16[2,2,258048]{2,1,0:T(2,128)(2,1)S(1)} %reshape.227), channel_id=1, replica_groups=mesh['lev'=2,'lon'=4,'lat'=4] {'lev'}, dimensions={0} | all-to-all | bytes 4128768 | tf_op jit(solution)/shard_map/all_to_all | solution.py:175
  602.9 5.6 reshape.228
  608.5 12.5 %copy.85 = bf16[21,6,64,2,64]{4,3,2,1,0:T(2,128)(2,1)} copy(bf16[21,6,64,2,64]{4,2,1,0,3:T(8,128)(2,1)} %bitcast.46) | data formatting | bytes 4128768 | tf_op jit(solution)/shard_map/all_to_all | solution.py:175
  621.0 6.9 reshape.197
  627.9 1.3 copy.86
  629.2 28.9 %all_to_all.57 = bf16[64,126,128]{2,1,0:T(8,128)(2,1)} all-to-all(bf16[64,126,128]{2,1,0:T(8,128)(2,1)S(1)} %copy.86), channel_id=1, replica_groups=mesh['lev'=2,'lon'=4,'lat'=4] {'lon'}, dimensions={0} | all-to-all | bytes 4128768 | tf_op jit(solution)/shard_map/all_to_all | solution.py:184
  658.1 3.2 copy.88
  661.3 0.8 fusion.19
  662.1 0.2 copy-done.6
  662.3 0.8 fusion
  663.0 1.8 copy.91
  664.9 5.0 all-to-all-start.3
  669.9 0.2 reduce-window.9
  670.0 0.1 reduce
  670.2 0.1 pad_maximum_fusion.1
  670.2 0.1 fusion.17
  670.3 0.1 fusion.16
  670.4 0.2 select_reduce_fusion
  670.6 0.7 exponential_multiply_fusion.diag_ref
  671.2 0.7 broadcast_in_dim.38.order_ref
  671.9 0.6 broadcast_in_dim.39.sin_ref
  672.5 5.3 legendre.1
  677.9 1.3 bitcast_convert_fusion
  679.2 1.3 fusion.1
  680.5 0.1 pad_maximum_fusion
  680.6 16.0 %all-to-all-done.3 = bf16[16,8,2,16,126]{4,3,2,1,0:T(8,128)(2,1)S(1)} async-done(((bf16[16,8,2,16,126]{4,3,2,1,0:T(8,128)(2,1)}), bf16[16,8,2,16,126]{4,3,2,1,0:T(8,128)(2,1)S(1)}, u32[]{:S(2)}, u32[]{:S(2)}) %all-to-all-start.3) | async-done | bytes 1032224 | tf_op jit(solution)/shard_map/all_to_all | solution.py:197
  696.7 0.9 copy.92
  697.6 0.7 reshape.199
  698.3 0.5 fusion.2
  698.8 0.1 slice_add_fusion
  699.0 0.6 copy.95
  699.6 1.1 copy.96
  (20 shorter events, 0.2 us)
Async XLA Ops:
  11.7 4.4 copy-start.7
  11.7 29.9 %all-to-all-start = ((bf16[2,2,258048]{2,1,0:T(2,128)(2,1)}), bf16[2,2,258048]{2,1,0:T(2,128)(2,1)S(1)}, u32[]{:S(2)}, u32[]{:S(2)}) async-start(bf16[2,2,258048]{2,1,0:T(2,128)(2,1)} %reshape.225), calls=%async_computation | async-start | bytes 4128768 | tf_op jit(solution)/shard_map/all_to_all | solution.py:167
  76.2 1.0 copy-start
  76.3 1.0 copy-start.1
  76.3 1.0 copy-start.2
  76.3 1.0 copy-start.3
  76.3 1.0 copy-start.4
  658.1 3.2 copy-start.5
  661.3 1.0 copy-start.6
  664.9 31.8 %all-to-all-start.3 = ((bf16[16,8,2,16,126]{4,3,2,1,0:T(8,128)(2,1)}), bf16[16,8,2,16,126]{4,3,2,1,0:T(8,128)(2,1)S(1)}, u32[]{:S(2)}, u32[]{:S(2)}) async-start(bf16[16,8,2,16,126]{4,3,2,1,0:T(8,128)(2,1)} %bitcast.15), calls=%async_computation.3 | async-start | bytes 2097152 | tf_op jit(solution)/shard_map/all_to_all | solution.py:197

commit v2 on v1

--- a/solution.py
+++ b/solution.py
@@ -72,10 +72,11 @@
     return jnp.cos(lat_angle) * math.sqrt(2.0 * math.pi / lat_count)
 
 
-def column_kernel(dil_ref, col_ref, lift_ref, conv_ref, bias_ref, out_w_ref, out_ref, ping, pong):
+def column_kernel(dil_ref, pair_ref, count_ref, col_ref, lift_ref, conv_ref, bias_ref, out_w_ref, out_ref, ping, pong):
     levels, _, tile = col_ref.shape
     channels = lift_ref.shape[1]
     layers = conv_ref.shape[0]
+    spare = levels + 3 * DMAX
 
     @pl.when(pl.program_id(0) == 0)
     def _():
@@ -83,6 +84,7 @@
         for buf in (ping, pong):
             buf[pl.ds(0, DMAX)] = edge
             buf[pl.ds(DMAX + levels, DMAX)] = edge
+            buf[pl.ds(2 * DMAX + levels, DMAX)] = edge
 
     lift = lift_ref[...]
 
@@ -100,10 +102,13 @@
         src, dst = (ping, pong) if layer % 2 == 0 else (pong, ping)
         spacing = dil_ref[layer]
 
-        def conv_level(lev, carry, src=src, dst=dst, spacing=spacing, layer=layer):
-            own = src[DMAX + lev]
+        def conv_pair(pair, carry, src=src, dst=dst, spacing=spacing, layer=layer):
+            low = pair_ref[layer, pair]
+            high = low + spacing
+            own_low = src[DMAX + low]
+            own_high = src[DMAX + high]
             taps = jnp.concatenate(
-                [src[DMAX + lev - spacing], own, src[DMAX + lev + spacing]], axis=1
+                [src[DMAX + low - spacing], own_low, own_high, src[DMAX + high + spacing]], axis=1
             )
             value = (
                 jnp.dot(taps, conv_ref[layer], preferred_element_type=jnp.float32)
@@ -111,18 +116,26 @@
             )
             curve = jnp.tanh(value * (inner + (inner * 0.044715) * (value * value)))
             half = 0.5 * value
-            fresh = (own.astype(jnp.float32) + (half + half * curve)).astype(jnp.bfloat16)
-            if layer + 1 < layers:
-                dst[DMAX + lev] = fresh
-            else:
-                correction = lax.dot_general(
-                    out_w_ref[...], fresh, (((1,), (1,)), ((), ())),
-                    preferred_element_type=jnp.float32,
-                )
-                out_ref[lev] = (col_ref[lev].astype(jnp.float32) + correction).astype(jnp.bfloat16)
+            gelu = half + half * curve
+            fresh_low = (own_low.astype(jnp.float32) + gelu[:, :channels]).astype(jnp.bfloat16)
+            fresh_high = (own_high.astype(jnp.float32) + gelu[:, channels:]).astype(jnp.bfloat16)
+            dst[DMAX + low] = fresh_low
+            dst[jnp.where(high < levels, DMAX + high, spare)] = fresh_high
             return carry
 
-        lax.fori_loop(0, levels, conv_level, 0)
+        lax.fori_loop(0, count_ref[layer], conv_pair, 0)
+
+    last = ping if layers % 2 == 0 else pong
+
+    def project_level(lev, carry):
+        correction = lax.dot_general(
+            out_w_ref[...], last[DMAX + lev], (((1,), (1,)), ((), ())),
+            preferred_element_type=jnp.float32,
+        )
+        out_ref[lev] = (col_ref[lev].astype(jnp.float32) + correction).astype(jnp.bfloat16)
+        return carry
+
+    lax.fori_loop(0, levels, project_level, 0)
 
 
 def column_net(col_flat, dilation, lift_weight, conv_weight, conv_bias, out_weight):
@@ -131,20 +144,29 @@
     tile = min(512, columns)
     while columns % tile:
         tile //= 2
-    whole = lambda *dims: pl.BlockSpec(dims, lambda i, d: (0,) * len(dims))
-    moving = pl.BlockSpec((levels, field_count, tile), lambda i, d: (0, 0, i))
-    scratch = pltpu.VMEM((levels + 2 * DMAX, tile, channels), jnp.bfloat16)
+    flat = conv_weight.reshape(layers, taps * channels, channels)
+    blank = jnp.zeros((layers, channels, channels), conv_weight.dtype)
+    paired = jnp.concatenate(
+        [jnp.concatenate([flat, blank], axis=1), jnp.concatenate([blank, flat], axis=1)], axis=2
+    )
+    level_ids = jnp.arange(levels, dtype=jnp.int32)[None, :]
+    is_low = (level_ids // dilation[:, None]) % 2 == 0
+    counts = jnp.sum(is_low.astype(jnp.int32), axis=1)
+    pairs = jnp.sort(jnp.where(is_low, level_ids, levels), axis=1)
+    whole = lambda *dims: pl.BlockSpec(dims, lambda i, *d: (0,) * len(dims))
+    moving = pl.BlockSpec((levels, field_count, tile), lambda i, *d: (0, 0, i))
+    scratch = pltpu.VMEM((levels + 3 * DMAX + 1, tile, channels), jnp.bfloat16)
     return pl.pallas_call(
         column_kernel,
         out_shape=jax.ShapeDtypeStruct(col_flat.shape, jnp.bfloat16),
         grid_spec=pltpu.PrefetchScalarGridSpec(
-            num_scalar_prefetch=1,
+            num_scalar_prefetch=3,
             grid=(columns // tile,),
             in_specs=[
                 moving,
                 whole(field_count, channels),
-                whole(layers, taps * channels, channels),
-                whole(layers, channels),
+                whole(layers, (taps + 1) * channels, 2 * channels),
+                whole(layers, 2 * channels),
                 whole(field_count, channels),
             ],
             out_specs=moving,
@@ -154,10 +176,12 @@
         name="column_net",
     )(
         dilation,
+        pairs,
+        counts,
         col_flat,
         lift_weight,
-        conv_weight.reshape(layers, taps * channels, channels),
-        conv_bias,
+        paired,
+        jnp.concatenate([conv_bias, conv_bias], axis=1),
         jnp.transpose(out_weight),
     )
 

time: 702 us -> 594 us (0.85)
  Pallas kernels: 478 us -> 372 us
    pallas_call x1, Pallas kernels: 472 us -> 366 us  [column_net(): pl.pallas_call(column_kernel, out_shape=jax.ShapeDtypeStruct(col_flat.sha...]
    unnamed x21 -> x23, local copies, waits for them, and re-layouts: 28.2 us -> 28 us
where the time goes in v2:
time: 594 us
  Pallas kernels  372 us (63%)
  local copies, waits for them, and re-layouts  109 us (18%)
  blocking collectives  56.5 us (10%)
  waiting for transfers between devices  41 us (7%)
  starting transfers between devices  9.33 us (2%)
    pallas_call x1, Pallas kernels, column_net(): pl.pallas_call(column_kernel, out_shape=jax.ShapeDtypeStruct(col_flat.sha...  366 us
    all_to_all x1, blocking collectives, on_device(): lax.all_to_all(rows, 'lon', split_axis=0, concat_axis=2, tiled=True)  28.9 us
    unnamed x23, local copies, waits for them, and re-layouts  28 us
    all_to_all x1, blocking collectives, on_device(): lax.all_to_all(slotted, 'lev', split_axis=0, concat_axis=3, tiled=True)  27.6 us
    all_to_all x1, waiting for transfers between devices, on_device(): lax.all_to_all(fields, 'lev', split_axis=3, concat_axis=0, tiled=True)  23.9 us
    all_to_all x2, local copies, waits for them, and re-layouts, on_device(): lax.all_to_all(fields, 'lev', split_axis=3, concat_axis=0, tiled=True)  18.6 us
    all_to_all x1, waiting for transfers between devices, on_device(): lax.all_to_all(fourier, ('lon', 'lat'), split_axis=0, concat_axis=0, tile...  17.1 us
    scatter x1, local copies, waits for them, and re-layouts, on_device(): jnp.zeros(received.shape, jnp.bfloat16).at[level_slot].set(corrected)  12.5 us
  transfers between devices with their start and end apart: 2, of which 2 were waited for; matrix products, arithmetic and copies ran while one was open for 1% of the time, Pallas kernels for 1%

profile of v2, /device:TPU:0, one launch (start us, length us, event | category | flops | bytes accessed | tf_op | source)
XLA Modules:
  0.0 594.5 jit_solution(8710097578774334384)
XLA Ops:
  0.0 6.2 %copy.82 = bf16[21,6,64,128]{2,0,1,3:T(8,128)(2,1)} copy(bf16[21,6,64,128]{3,2,1,0:T(8,128)(2,1)} %param.9) | data formatting | bytes 4128768 | tf_op args[0]
  6.2 5.5 reshape.233
  11.7 4.4 all-to-all-start
  16.1 0.3 convert_reduce_fusion
  16.4 1.0 sort.14
  17.5 0.1 fusion.3.conv_ref
  17.6 23.9 %all-to-all-done = bf16[2,2,258048]{2,1,0:T(2,128)(2,1)S(1)} async-done(((bf16[2,2,258048]{2,1,0:T(2,128)(2,1)}), bf16[2,2,258048]{2,1,0:T(2,128)(2,1)S(1)}, u32[]{:S(2)}, u32[]{:S(2)}) %all-to-all-start) | async-done | bytes 2064416 | tf_op jit(solution)/shard_map/all_to_all | solution.py:191
  41.6 5.3 reshape.234
  46.9 13.4 %copy.105 = bf16[21,6,64,2,64]{4,3,2,1,0:T(2,128)(2,1)} copy(bf16[21,6,64,2,64]{2,0,1,4,3:T(8,128)(2,1)} %bitcast.41) | data formatting | bytes 4128768 | tf_op jit(solution)/shard_map/all_to_all | solution.py:191
  60.3 5.2 copy.84
  65.5 5.3 gather_fusion
  70.8 5.3 reshape.230
  76.2 0.4 broadcast_select_fusion.col_ref
  76.5 0.3 copy-done
  76.8 366.5 %column_net.1 = bf16[37,6,4096]{2,1,0:T(8,128)(2,1)S(1)} custom-call(s32[4]{0:T(128)S(1)} %copy-done.2, s32[4,37]{1,0:T(4,128)S(1)} %copy.87.pair_ref, s32[4]{0:T(128)S(1)} %get-tuple-element.8.count_ref, bf16[37,6,4096]{2,1,0:T(8,128)(2,1)S(1)} %broadcast_select_fusion.col_ref, bf16[6,128]{1,0:T(8,128)(2,1)S(1)} %copy-done, ...), custom_call_target="tpu_custom_call" | custom-call | tf_op jit(solution)/shard_map/column_net/pallas_call | solution.py:159
  443.3 5.5 reshape.231
  448.9 3.0 broadcast_in_dim.28
  451.9 12.5 %scatter_fusion = bf16[42,6,64,64]{3,2,1,0:T(8,128)(2,1)} fusion(bf16[42,6,64,64]{3,2,1,0:T(8,128)(2,1)} %broadcast_in_dim.28, s32[37]{0:T(128)S(1)} %compare_select_fusion, bf16[37,6,64,64]{3,2,1,0:T(8,128)(2,1)} %reshape.231), kind=kCustom, calls=%fused_computation.1 | custom fusion | bytes 5456020 | tf_op jit(solution)/shard_map/scatter | solution.py:198
  464.4 4.8 reshape.235
  469.2 27.6 %all_to_all.56 = bf16[2,2,258048]{2,1,0:T(2,128)(2,1)} all-to-all(bf16[2,2,258048]{2,1,0:T(2,128)(2,1)S(1)} %reshape.235), channel_id=1, replica_groups=mesh['lev'=2,'lon'=4,'lat'=4] {'lev'}, dimensions={0} | all-to-all | bytes 4128768 | tf_op jit(solution)/shard_map/all_to_all | solution.py:199
  496.8 5.6 reshape.236
  502.3 12.5 %copy.90 = bf16[21,6,64,2,64]{4,3,2,1,0:T(2,128)(2,1)} copy(bf16[21,6,64,2,64]{4,2,1,0,3:T(8,128)(2,1)} %bitcast.45) | data formatting | bytes 4128768 | tf_op jit(solution)/shard_map/all_to_all | solution.py:199
  514.8 6.9 %reshape.205 = bf16[126,64,128]{2,1,0:T(8,128)(2,1)S(1)} reshape(bf16[21,6,64,2,64]{4,3,2,1,0:T(2,128)(2,1)} %copy.90) | data formatting | bytes 4128768 | tf_op jit(solution)/shard_map/reshape | solution.py:206
  521.7 1.3 copy.91
  523.0 28.9 %all_to_all.57 = bf16[64,126,128]{2,1,0:T(8,128)(2,1)} all-to-all(bf16[64,126,128]{2,1,0:T(8,128)(2,1)S(1)} %copy.91), channel_id=1, replica_groups=mesh['lev'=2,'lon'=4,'lat'=4] {'lon'}, dimensions={0} | all-to-all | bytes 4128768 | tf_op jit(solution)/shard_map/all_to_all | solution.py:208
  551.9 3.2 copy.93
  555.1 0.8 fusion.25
  555.9 0.2 copy-done.6
  556.1 0.8 fusion.2
  556.9 1.9 copy.96
  558.7 5.0 all-to-all-start.3
  563.7 0.2 reduce-window.9
  563.9 0.1 reduce
  564.2 0.2 select_reduce_fusion
  564.4 0.7 exponential_multiply_fusion.diag_ref
  565.1 0.7 broadcast_in_dim.52.order_ref
  565.7 0.6 broadcast_in_dim.53.sin_ref
  566.3 5.3 legendre.1
  571.7 1.4 bitcast_convert_fusion
  573.1 0.1 copy-done.3
  573.2 0.1 fusion.4
  573.4 17.1 %all-to-all-done.3 = bf16[16,8,2,16,126]{4,3,2,1,0:T(8,128)(2,1)S(1)} async-done(((bf16[16,8,2,16,126]{4,3,2,1,0:T(8,128)(2,1)}), bf16[16,8,2,16,126]{4,3,2,1,0:T(8,128)(2,1)S(1)}, u32[]{:S(2)}, u32[]{:S(2)}) %all-to-all-start.3) | async-done | bytes 1032224 | tf_op jit(solution)/shard_map/all_to_all | solution.py:221
  590.5 0.9 copy.97
  591.5 0.7 reshape.207
  592.1 0.5 fusion.5
  592.7 0.1 slice_add_fusion
  592.8 0.6 copy.100
  593.4 1.1 copy.101
  (30 shorter events, 0.5 us)
Async XLA Ops:
  11.7 4.4 copy-start.2
  11.7 5.8 copy-start.8
  11.7 5.8 copy-start.7
  11.7 5.8 copy-start.4
  11.7 29.9 %all-to-all-start = ((bf16[2,2,258048]{2,1,0:T(2,128)(2,1)}), bf16[2,2,258048]{2,1,0:T(2,128)(2,1)S(1)}, u32[]{:S(2)}, u32[]{:S(2)}) async-start(bf16[2,2,258048]{2,1,0:T(2,128)(2,1)} %reshape.233), calls=%async_computation | async-start | bytes 4128768 | tf_op jit(solution)/shard_map/all_to_all | solution.py:191
  76.1 0.7 copy-start
  76.2 0.7 copy-start.1
  551.9 3.2 copy-start.5
  555.1 1.0 copy-start.6
  558.7 31.8 %all-to-all-start.3 = ((bf16[16,8,2,16,126]{4,3,2,1,0:T(8,128)(2,1)}), bf16[16,8,2,16,126]{4,3,2,1,0:T(8,128)(2,1)S(1)}, u32[]{:S(2)}, u32[]{:S(2)}) async-start(bf16[16,8,2,16,126]{4,3,2,1,0:T(8,128)(2,1)} %bitcast.15), calls=%async_computation.3 | async-start | bytes 2097152 | tf_op jit(solution)/shard_map/all_to_all | solution.py:221
  571.7 1.5 copy-start.3
